TPU v7x, 512 devices: a whole 4x4x16 slice. The times are simulated.
512 devices in a mesh: seq: 64 (over y, z), mp: 8 (over x, core).
Axes of the slice: x: 4, y: 4, z: 16, core: 2. Of those that a mesh axis runs over, the one named last changes fastest.
Arguments:
- byte_states: bfloat16 [16384, 1024], P('seq'), may hold values from -6 to 6
- outer_gain: float32 [1024], replicated, may hold values from 0.1 to 1.9
- mamba_input: bfloat16 [1024, 1024], P(None, 'mp'), may hold values from -0.1875 to 0.1875
- mamba_step: bfloat16 [1024, 1024], P(None, 'mp'), may hold values from -0.1875 to 0.1875
- decay_rate: float32 [1024], P('mp'), as said below
- mixer_weight: bfloat16 [1024, 1024], P('mp'), may hold values from -0.1875 to 0.1875
- boundaries: int32 [64, 128], P('seq'), may hold values from 0 to 256, as said below
- span_counts: int32 [64], replicated, may hold values from 1 to 128, as said below
- up_weight: bfloat16 [1024, 4096], P('seq', 'mp'), may hold values from -0.1875 to 0.1875
- up_bias: float32 [4096], P('mp'), may hold values from -5 to 5
- inner_gain: float32 [4096], replicated, as said below
- query_weight: bfloat16 [4096, 4096], P('seq', 'mp'), as said below
- key_weight: bfloat16 [4096, 1024], P('seq', 'mp'), as said below
- value_weight: bfloat16 [4096, 1024], P('seq', 'mp'), may hold values from -0.09375 to 0.09375
- return_weight: bfloat16 [4096, 1024], P('mp'), may hold values from -0.09375 to 0.09375
Outputs:
- joined: bfloat16 [16384, 1024], P('seq', 'mp')
Inputs may be any that keep to these rules, and one draw needn't show every extreme that they name: `boundaries`: row s lists the spans of shard s: its first span_counts[s] entries rise strictly from 0 and are byte positions within the shard; each span runs to the next entry, the last to the shard's end; the other entries equal 256. `span_counts`: the counts sum to 4096; some shard has exactly 128 spans. `decay_rate`: Positive. `inner_gain`: Positive. `query_weight`: Finite. `key_weight`: Finite.
All inputs are finite; a program needn't handle non-finite values.
Results may differ from a plain program's by a relative error of at most 0.01.
Values may be sent and summed in bfloat16 or wider, within the bound.
A program may use at most 64 MiB of HBM per device.

v0:
```python
import math

import jax
import jax.numpy as jnp
from jax import lax
from jax.sharding import PartitionSpec as P

HEADS = 32
KV_HEADS = 8
HEAD = 128


eps = 1e-05
masked = -1e30
far_index = 1073741824


def prefix(value, axis, join, neutral):
    count, mine = (lax.axis_size(axis), lax.axis_index(axis))
    pieces = jax.tree.map(lambda part: lax.all_gather(part, axis), value)
    so_far = jax.tree.map(
        lambda part, zero: jnp.full_like(part, 0) + jnp.asarray(zero, part.dtype), value, neutral
    )

    def lap(position, so_far):
        longer = join(so_far, jax.tree.map(lambda part: part[position], pieces))
        return jax.tree.map(lambda new, old: jnp.where(position < mine, new, old), longer, so_far)

    return lax.fori_loop(0, count - 1, lap, so_far)


def rms_scale(values, gain):
    values = values.astype(jnp.float32)
    return values * lax.rsqrt(jnp.mean(values * values, axis=-1, keepdims=True) + eps) * gain


def combine_pairs(earlier, later):
    return (earlier[0] * later[0], later[0] * earlier[1] + later[1])


def pick_table(table, wanted, seq_ids):
    return jnp.sum(jnp.where(seq_ids[None, :] == wanted[:, None], table[None, :], 0), axis=1)


def block_size(piece_rows, shard_rows):
    limit = max(1, 1024 // shard_rows)
    pieces = max(1, piece_rows // shard_rows)
    best_size = 1
    for candidate in range(1, limit + 1):
        if pieces % candidate == 0:
            best_size = candidate
    return min(piece_rows, best_size * shard_rows)


def on_device(
    byte_states,
    outer_gain,
    mamba_input,
    mamba_step,
    decay_rate,
    mixer_weight,
    boundaries,
    span_counts,
    up_weight,
    up_bias,
    inner_gain,
    query_weight,
    key_weight,
    value_weight,
    return_weight,
):
    shards = lax.axis_size("seq")
    own_shard = lax.axis_index("seq")
    own_lane = lax.axis_index("mp")
    rows_here = byte_states.shape[0]
    capacity = boundaries.shape[1]
    column_count = mamba_input.shape[1]
    kv_local = key_weight.shape[1] // HEAD
    group_size = HEADS // KV_HEADS
    offsets = jnp.cumsum(span_counts) - span_counts
    seq_ids = jnp.arange(shards, dtype=jnp.int32)
    own_offset = jnp.sum(jnp.where(seq_ids == own_shard, offsets, 0))
    own_count = jnp.sum(jnp.where(seq_ids == own_shard, span_counts, 0))
    normed = rms_scale(byte_states, outer_gain).astype(jnp.bfloat16)
    inputs = jnp.dot(normed, mamba_input, preferred_element_type=jnp.float32)
    step_sizes = jax.nn.softplus(jnp.dot(normed, mamba_step, preferred_element_type=jnp.float32))
    rate_steps = step_sizes * decay_rate
    decays = jnp.exp(-rate_steps)
    drives = jnp.sqrt(-jnp.expm1(-2.0 * rate_steps)) * inputs
    through, local_states = lax.associative_scan(combine_pairs, (decays, drives), axis=0)
    starting = (jnp.ones((column_count,), jnp.float32), jnp.zeros((column_count,), jnp.float32))
    arriving = prefix((through[-1], local_states[-1]), "seq", combine_pairs, starting)
    states = (local_states + through * arriving[1][None, :]).astype(jnp.bfloat16)
    partial_value = jnp.dot(states, mixer_weight, preferred_element_type=jnp.float32)
    mixed_sum = lax.psum(partial_value, "mp")
    encoded = (byte_states.astype(jnp.float32) + mixed_sum).astype(jnp.bfloat16)
    skip_part = lax.dynamic_slice_in_dim(encoded, own_lane * column_count, column_count, 1)
    own_marks = boundaries[0]
    pooled = encoded[jnp.minimum(own_marks, rows_here - 1)]
    local_slot = jnp.arange(capacity, dtype=jnp.int32)
    query_index = jnp.where(local_slot < own_count, own_offset + local_slot, -1)
    columns = pooled
    widened_sum = jnp.dot(
        columns,
        lax.all_gather(up_weight, "seq", axis=0, tiled=True),
        preferred_element_type=jnp.float32,
    )
    widened_share = (widened_sum + up_bias[None, :]).astype(jnp.bfloat16)
    widened = lax.all_gather(widened_share, "mp", axis=1, tiled=True)
    inner_normed = rms_scale(widened, inner_gain).astype(jnp.bfloat16)
    columns = inner_normed
    query_part = jnp.dot(
        columns,
        lax.all_gather(query_weight, "seq", axis=0, tiled=True),
        preferred_element_type=jnp.float32,
    )
    key_part = jnp.dot(
        columns,
        lax.all_gather(key_weight, "seq", axis=0, tiled=True),
        preferred_element_type=jnp.float32,
    )
    value_part = jnp.dot(
        columns,
        lax.all_gather(value_weight, "seq", axis=0, tiled=True),
        preferred_element_type=jnp.float32,
    )
    queries = query_part.astype(jnp.bfloat16)
    key_rows = key_part.astype(jnp.bfloat16)
    value_rows = value_part.astype(jnp.bfloat16)
    query_count = queries.shape[0]
    grouped = (
        queries.reshape(query_count, kv_local, group_size, HEAD)
        .transpose(1, 0, 2, 3)
        .reshape(kv_local, query_count * group_size, HEAD)
    )
    row_index = jnp.repeat(query_index, group_size)
    shard_rows = key_rows.shape[0]
    score_scale = 1.0 / math.sqrt(HEAD)

    def key_index(whole_index):
        holder = whole_index // shard_rows
        within = whole_index % shard_rows
        holder_offset = pick_table(offsets, holder, seq_ids)
        holder_count = pick_table(span_counts, holder, seq_ids)
        return jnp.where(within < holder_count, holder_offset + within, far_index)

    def attend_block(running, key_block, value_block, index_block):
        row_peak, denominator, weighted = running
        scores = (
            jnp.einsum("hqd,khd->hqk", grouped, key_block, preferred_element_type=jnp.float32)
            * score_scale
        )
        scores = jnp.where(index_block[None, None, :] <= row_index[None, :, None], scores, masked)
        new_peak = jnp.maximum(row_peak, jnp.max(scores, axis=2))
        shrink = jnp.exp(row_peak - new_peak)
        lifted = jnp.exp(scores - new_peak[:, :, None])
        denominator = denominator * shrink + jnp.sum(lifted, axis=2)
        weighted = weighted * shrink[:, :, None] + jnp.einsum(
            "hqk,khd->hqd",
            lifted.astype(jnp.bfloat16),
            value_block,
            preferred_element_type=jnp.float32,
        )
        return (new_peak, denominator, weighted)

    query_total = query_count * group_size
    initial = (
        jnp.full((kv_local, query_total), masked, jnp.float32),
        jnp.zeros((kv_local, query_total), jnp.float32),
        jnp.zeros((kv_local, query_total, HEAD), jnp.float32),
    )
    key_piece = lax.all_gather(key_rows, "seq", axis=0, tiled=True)
    value_piece = lax.all_gather(value_rows, "seq", axis=0, tiled=True)
    piece_rows = key_piece.shape[0]
    block_rows = block_size(piece_rows, shard_rows)
    turn_count = piece_rows // block_rows
    key_blocks = key_piece.reshape(turn_count, block_rows, kv_local, HEAD)
    value_blocks = value_piece.reshape(turn_count, block_rows, kv_local, HEAD)

    def one_turn(turn_index, inner_running):
        whole_index = turn_index * block_rows + jnp.arange(block_rows, dtype=jnp.int32)
        return attend_block(
            inner_running, key_blocks[turn_index], value_blocks[turn_index], key_index(whole_index)
        )

    row_peak, denominator, weighted = lax.fori_loop(0, turn_count, one_turn, initial)
    attended = (weighted / denominator[:, :, None]).astype(jnp.bfloat16)
    attended = (
        attended.reshape(kv_local, query_count, group_size, HEAD)
        .transpose(1, 0, 2, 3)
        .reshape(query_count, kv_local * group_size * HEAD)
    )
    projected = jnp.dot(attended, return_weight, preferred_element_type=jnp.float32)
    returned = lax.psum_scatter(
        projected.astype(jnp.bfloat16), "mp", scatter_dimension=1, tiled=True
    )
    positions = jnp.arange(rows_here, dtype=jnp.int32)
    live_slots = jnp.arange(capacity, dtype=jnp.int32) < own_count
    passed = jnp.sum(
        ((own_marks[None, :] <= positions[:, None]) & live_slots[None, :]).astype(jnp.int32), axis=1
    )
    return (skip_part.astype(jnp.float32) + returned[passed - 1].astype(jnp.float32)).astype(
        jnp.bfloat16
    )


def solution(mesh):
    in_specs = (
        P("seq", None),
        P(),
        P(None, "mp"),
        P(None, "mp"),
        P("mp"),
        P("mp", None),
        P("seq", None),
        P(),
        P("seq", "mp"),
        P("mp"),
        P(),
        P("seq", "mp"),
        P("seq", "mp"),
        P("seq", "mp"),
        P("mp", None),
    )
    out_specs = P("seq", "mp")
    return jax.shard_map(
        on_device, mesh=mesh, in_specs=in_specs, out_specs=out_specs, check_vma=False
    )
```

profile of v0, /device:TPU:25, one launch (start us, length us, event | category | flops | bytes accessed | tf_op | source)
XLA Modules:
  0.0 1136.6 jit_solution(18261109659851616036)
XLA Ops:
  8.8 1.5 negate_exponential_fusion
  12.6 61.6 %all-gather.1 = f32[64,1,128]{2,1,0:T(1,128)S(1)} all-gather(f32[1,1,128]{2,1,0:T(1,128)S(1)} %add_bitcast_fusion), channel_id=1, replica_groups=mesh['seq'=64,'mp'=8] {'seq'}, dimensions={0}, use_global_device_ids=true | all-gather | bytes 33280 | tf_op jit(solution)/shard_map/all_gather | solution.py:20
  74.2 54.5 %all-gather = f32[64,1,128]{2,1,0:T(1,128)S(1)} all-gather(f32[1,1,128]{2,1,0:T(1,128)S(1)} %add_bitcast_fusion.1), channel_id=1, replica_groups=mesh['seq'=64,'mp'=8] {'seq'}, dimensions={0}, use_global_device_ids=true | all-gather | bytes 33280 | tf_op jit(solution)/shard_map/all_gather | solution.py:20
  128.8 2.6 while.34
  133.4 107.6 %all-reduce.34.cloned.1.call-done = f32[256,1024]{1,0:T(8,128)} async-done(((f32[256,1024]{1,0:T(8,128)}), f32[256,1024]{1,0:T(8,128)}) %all-reduce.34.cloned.1.call-update) | async-done | bytes 1048592 | tf_op jit(solution)/shard_map/psum | solution.py:95
  243.3 53.1 %all-gather.10.cloned.1.call-done = bf16[1024,512]{1,0:T(8,128)(2,1)} async-done(((bf16[16,512]{1,0:T(8,128)(2,1)}), bf16[1024,512]{1,0:T(8,128)(2,1)}) %all-gather.10.cloned.1.call-update) | async-done | bytes 1048592 | tf_op jit(solution)/shard_map/all_gather | solution.py:105
  296.3 2.2 fusion.31
  300.5 36.9 %all-gather.12.cloned.1.call-done = bf16[128,4096]{1,0:T(8,128)(2,1)} async-done(((bf16[128,512]{1,0:T(8,128)(2,1)}), bf16[128,4096]{1,0:T(8,128)(2,1)}) %all-gather.12.cloned.1.call-update) | async-done | bytes 1048592 | tf_op jit(solution)/shard_map/all_gather | solution.py:109
  337.3 1.6 fusion.28
  339.0 129.5 %all-gather.20.cloned.1.call-done = bf16[4096,128]{1,0:T(8,128)(2,1)} async-done(((bf16[64,128]{1,0:T(8,128)(2,1)}), bf16[4096,128]{1,0:T(8,128)(2,1)}) %all-gather.20.cloned.1.call-update) | async-done | bytes 1048592 | tf_op jit(solution)/shard_map/all_gather | solution.py:124
  468.5 2.7 convolution_convert_fusion.2
  471.3 136.0 %all-gather.14.cloned.1.call-done = bf16[4096,128]{1,0:T(8,128)(2,1)} async-done(((bf16[64,128]{1,0:T(8,128)(2,1)}), bf16[4096,128]{1,0:T(8,128)(2,1)}) %all-gather.14.cloned.1.call-update) | async-done | bytes 1048592 | tf_op jit(solution)/shard_map/all_gather | solution.py:119
  607.3 2.4 convolution_convert_fusion.3
  612.0 1.9 add_select_fusion.3
  614.6 138.0 %all-gather.18.cloned.1.call-done = bf16[4096,512]{1,0:T(8,128)(2,1)} async-done(((bf16[64,512]{1,0:T(8,128)(2,1)}), bf16[4096,512]{1,0:T(8,128)(2,1)}) %all-gather.18.cloned.1.call-update) | async-done | bytes 4194320 | tf_op jit(solution)/shard_map/all_gather | solution.py:114
  752.6 3.0 convolution_convert_fusion.1
  755.7 135.8 %all-gather.22.cloned.1.call-done = bf16[8192,128]{1,0:T(8,128)(2,1)} async-done(((bf16[128,128]{1,0:T(8,128)(2,1)}), bf16[8192,128]{1,0:T(8,128)(2,1)}) %all-gather.22.cloned.1.call-update) | async-done | bytes 2097168 | tf_op jit(solution)/shard_map/all_gather | solution.py:173
  891.5 140.0 %all-gather.16.cloned.1.call-done = bf16[8192,128]{1,0:T(8,128)(2,1)} async-done(((bf16[128,128]{1,0:T(8,128)(2,1)}), bf16[8192,128]{1,0:T(8,128)(2,1)}) %all-gather.16.cloned.1.call-update) | async-done | bytes 2097168 | tf_op jit(solution)/shard_map/all_gather | solution.py:172
  1031.5 50.0 %while.35 = (s32[]{:T(128)}, f32[1,512]{1,0:T(1,128)S(1)}, f32[1,512]{1,0:T(1,128)S(1)}, f32[1,512,128]{2,1,0:T(8,128)S(1)}, s32[64]{0:T(128)S(1)}, /*index=5*/s...) while((s32[]{:T(128)}, f32[1,512]{1,0:T(1,128)S(1)}, ...), condition=%wide.region_13.14_spmd.clone, body=%wide.region_8.13_spmd.clone.sunk | while | flops 273186304 | bytes 7548097 | solution.py:186
  1033.2 2.0 fusion.78
  1036.3 1.5 fusion.82
  1039.4 2.0 fusion.78
  1042.5 1.5 fusion.82
  1045.7 2.0 fusion.78
  1051.9 2.0 fusion.78
  1058.2 2.0 fusion.78
  1064.4 2.0 fusion.78
  1070.7 2.0 fusion.78
  1073.7 1.5 fusion.82
  1076.9 2.0 fusion.78
  1083.0 43.0 %reduce-scatter.4.cloned.1.call-done = bf16[128,128]{1,0:T(8,128)(2,1)} async-done(((bf16[1024,128]{1,0:T(8,128)(2,1)}), bf16[128,128]{1,0:T(8,128)(2,1)}) %reduce-scatter.4.cloned.1.call-update) | async-done | bytes 32784
  1127.7 1.5 add_convert_fusion
  (351 shorter events, 45.8 us)
Async XLA Ops:
  7.4 1074.4 %copy-start = (bf16[512,1024]{1,0:T(8,128)(2,1)S(1)}, bf16[512,1024]{1,0:T(8,128)(2,1)}, u32[]{:S(2)}) copy-start(bf16[512,1024]{1,0:T(8,128)(2,1)} %param.33) | copy-start | bytes 3145732
  7.4 3.0 copy-start.2
  7.4 3.0 copy-start.12
  7.4 3.0 copy-start.10
  7.4 233.6 %all-reduce.34.cloned.1.call-start = ((), (), s32[]{:S(2)}) async-start(), calls=%async_computation.1 | async-start | bytes 2097152 | tf_op jit(solution)/shard_map/psum | solution.py:95
  11.7 119.7 %copy-start.4 = (bf16[128,1024]{1,0:T(8,128)(2,1)S(1)}, bf16[128,1024]{1,0:T(8,128)(2,1)}, u32[]{:S(2)}) copy-start(bf16[128,1024]{1,0:T(8,128)(2,1)} %param.24) | copy-start | bytes 786436
  12.5 120.8 %copy-start.9 = (s32[1,128]{1,0:T(1,128)S(1)}, s32[1,128]{1,0:T(1,128)}, u32[]{:S(2)}) copy-start(s32[1,128]{1,0:T(1,128)} %param.25) | copy-start | bytes 1540
  132.7 163.6 %all-gather.10.cloned.1.call-start = ((), (), s32[]{:S(2)}) async-start(), calls=%async_computation.2 | async-start | bytes 1064960 | tf_op jit(solution)/shard_map/all_gather | solution.py:105
  133.3 204.1 %all-gather.12.cloned.1.call-start = ((), (), s32[]{:S(2)}) async-start(), calls=%async_computation.3 | async-start | bytes 1179648 | tf_op jit(solution)/shard_map/all_gather | solution.py:109
  133.3 163.0 %copy-start.8 = (f32[512]{0:T(512)S(1)}, f32[512]{0:T(512)}, u32[]{:S(2)}) copy-start(f32[512]{0:T(512)} %param.28) | copy-start | bytes 6148
  242.4 96.6 %copy-start.1 = (bf16[256,1024]{1,0:T(8,128)(2,1)}, bf16[256,1024]{1,0:T(8,128)(2,1)S(1)}, u32[]{:S(2)}) copy-start(bf16[256,1024]{1,0:T(8,128)(2,1)S(1)} %fusion.35) | copy-start | bytes 1572868
  242.4 226.1 %copy-start.11 = (f32[4096]{0:T(1024)S(1)}, f32[4096]{0:T(1024)}, u32[]{:S(2)}) copy-start(f32[4096]{0:T(1024)} %param.29) | copy-start | bytes 49156
  298.5 170.0 %all-gather.20.cloned.1.call-start = ((), (), s32[]{:S(2)}) async-start(), calls=%async_computation.7 | async-start | bytes 1064960 | tf_op jit(solution)/shard_map/all_gather | solution.py:124
  299.3 308.0 %all-gather.14.cloned.1.call-start = ((), (), s32[]{:S(2)}) async-start(), calls=%async_computation.4 | async-start | bytes 1064960 | tf_op jit(solution)/shard_map/all_gather | solution.py:119
  299.9 452.8 %all-gather.18.cloned.1.call-start = ((), (), s32[]{:S(2)}) async-start(), calls=%async_computation.6 | async-start | bytes 4259840 | tf_op jit(solution)/shard_map/all_gather | solution.py:114
  300.4 591.1 %all-gather.22.cloned.1.call-start = ((), (), s32[]{:S(2)}) async-start(), calls=%async_computation.8 | async-start | bytes 2129920 | tf_op jit(solution)/shard_map/all_gather | solution.py:173
  337.3 270.0 %copy-start.3 = (bf16[128,4096]{1,0:T(8,128)(2,1)S(1)}, bf16[128,4096]{1,0:T(8,128)(2,1)}, u32[]{:S(2)}) copy-start(bf16[128,4096]{1,0:T(8,128)(2,1)} %all-gather.12.cloned.1.call-done) | copy-start | bytes 3145732
  339.0 270.8 %copy-start.5 = (s32[64]{0:T(128)S(1)}, s32[64]{0:T(128)}, u32[]{:S(2)}) copy-start(s32[64]{0:T(128)} %param.26) | copy-start | bytes 772
  471.2 560.3 %all-gather.16.cloned.1.call-start = ((), (), s32[]{:S(2)}) async-start(), calls=%async_computation.5 | async-start | bytes 2129920 | tf_op jit(solution)/shard_map/all_gather | solution.py:172
  609.7 516.2 %reduce-scatter.4.cloned.1.call-start = ((), (), s32[]{:S(2)}) async-start(), calls=%async_computation.9 | async-start | bytes 294912
  1035.9 1.9 copy-start.6
  1042.1 1.9 copy-start.6
  1048.4 1.9 copy-start.6
  1054.6 1.9 copy-start.6
  1060.9 1.9 copy-start.6
  1067.1 1.9 copy-start.6
  1073.4 1.9 copy-start.6
  1079.6 1.9 copy-start.6
  1081.5 1.4 copy-start.7
Sparse Core Ops, SparseCore 0:
  132.8 108.1 all-reduce.33
  298.7 38.6 all-gather.11
  340.3 128.1 all-gather.19
  471.3 135.9 all-gather.13
  610.1 142.4 all-gather.17
  755.4 136.0 all-gather.21
  894.5 137.0 all-gather.15
  1083.0 42.8 reduce-scatter.3
Sparse Core Ops, SparseCore 1:
  136.1 160.2 all-gather.9
where the time goes:
time: 1140 us
  waiting for transfers between devices  922 us (81%)
  blocking collectives  116 us (10%)
  matrix products  41.2 us (4%)
  other arithmetic  27.3 us (2%)
  between operations  15.9 us (1%)
  local copies, waits for them, and re-layouts  11.6 us (1%)
    all_gather x1, waiting for transfers between devices, on_device(): key_piece = lax.all_gather(key_rows, 'seq', axis=0, tiled=True)  140 us
    all_gather x1, waiting for transfers between devices, on_device(): lax.all_gather(query_weight, 'seq', axis=0, tiled=True)  138 us
    all_gather x1, waiting for transfers between devices, on_device(): lax.all_gather(key_weight, 'seq', axis=0, tiled=True)  136 us
    all_gather x1, waiting for transfers between devices, on_device(): value_piece = lax.all_gather(value_rows, 'seq', axis=0, tiled=True)  136 us
    all_gather x1, waiting for transfers between devices, on_device(): lax.all_gather(value_weight, 'seq', axis=0, tiled=True)  130 us
    all_gather x2, blocking collectives, prefix(): pieces = jax.tree.map(lambda part: lax.all_gather(part, axis), value)  116 us
    psum x1, waiting for transfers between devices, on_device(): mixed_sum = lax.psum(partial_value, 'mp')  108 us
    all_gather x1, waiting for transfers between devices, on_device(): lax.all_gather(up_weight, 'seq', axis=0, tiled=True)  53.1 us
  transfers between devices with their start and end apart: 9, of which 9 were waited for; matrix products, arithmetic and copies ran while one was open for 1% of the time, Pallas kernels for 0%

commit v1 on v0

v1 whole, which is shorter than its diff:
```python
import math

import jax
import jax.numpy as jnp
from jax import lax
from jax.experimental import pallas as pl
from jax.experimental.pallas import tpu as pltpu
from jax.sharding import PartitionSpec as P

HEADS = 32
KV_HEADS = 8
HEAD = 128
NY, NZ = 4, 16
NX, NC = 4, 2
CAP = 128
KV_A = 48

eps = 1e-05
masked = -1e30
far_index = 1073741824

MESH = pl.DeviceIdType.MESH
VM = pl.BlockSpec(memory_space=pltpu.VMEM)
DMA = pltpu.SemaphoreType.DMA


def coords():
    s, m = lax.axis_index("seq"), lax.axis_index("mp")
    return s // NZ, s % NZ, m // NC, m % NC


def remote(src, dst, ss, rs, y, z, m):
    return pltpu.make_async_remote_copy(
        src_ref=src, dst_ref=dst, send_sem=ss, recv_sem=rs, device_id=(y * NZ + z, m), device_id_type=MESH
    )


def enter(peers):
    barrier = pltpu.get_barrier_semaphore()
    for seq, mp in peers:
        pl.semaphore_signal(barrier, inc=1, device_id=(seq, mp), device_id_type=MESH)
    pl.semaphore_wait(barrier, len(peers))


def yz_peers(y, z, m):
    return [
        (y * NZ + (z + 1) % NZ, m),
        (y * NZ + (z + NZ - 1) % NZ, m),
        ((y + 1) % NY * NZ + z, m),
        ((y + NY - 1) % NY * NZ + z, m),
    ]


def mp_peers(s, x, c):
    same = [(s, ((x + k) % NX) * NC + c) for k in range(1, NX)]
    return same + [(s, x * NC + 1 - c)]


class RingY:
    def __init__(self, buf, ss, rs, cut, place):
        self.buf, self.ss, self.rs, self.cut = buf, ss, rs, cut
        self.y, self.z, self.m = place

    def part(self, yy, zz, k):
        ref = self.buf.at[yy % NY, zz]
        rows = self.buf.shape[2]
        if k == 2:
            return ref.at[pl.ds(0, self.cut)]
        if k == 3:
            return ref.at[pl.ds(self.cut, rows - self.cut)]
        return ref

    def copy(self, k, yy, zz, src=None):
        up = k in (0, 2)
        ref = self.part(yy, zz, k)
        return remote(
            ref if src is None else src,
            ref,
            self.ss.at[k, zz],
            self.rs.at[k, zz],
            (self.y + (1 if up else NY - 1)) % NY,
            self.z,
            self.m,
        )

    def start(self, zz, src=None):
        self.copy(0, self.y, zz, src).start()
        self.copy(1, self.y, zz, src).start()

    def relay(self, zz):
        self.copy(0, self.y + NY - 1, zz).wait_recv()
        self.copy(2, self.y + NY - 1, zz).start()
        self.copy(1, self.y + 1, zz).wait_recv()
        self.copy(3, self.y + 1, zz).start()

    def finish(self, zz):
        self.copy(2, self.y + 2, zz).wait_recv()
        self.copy(3, self.y + 2, zz).wait_recv()

    def drain(self, zz):
        for k, yy in ((0, self.y), (1, self.y), (2, self.y + NY - 1), (3, self.y + 1)):
            self.copy(k, yy, zz).wait_send()


class RingZ:
    def __init__(self, view, ss, rs, place):
        self.view, self.ss, self.rs = view, ss, rs
        self.y, self.z, self.m = place

    def item(self, d, t):
        return (self.z + (NZ - t if d == 0 else t)) % NZ

    def copy(self, d, t, zz, src=None):
        ref = self.view(zz)
        return remote(
            ref if src is None else src,
            ref,
            self.ss.at[d, t],
            self.rs.at[d, t],
            self.y,
            (self.z + (1 if d == 0 else NZ - 1)) % NZ,
            self.m,
        )

    def send(self, d, t, src=None):
        self.copy(d, t, self.item(d, t), src).start()

    def arrive(self, d, t):
        self.copy(d, t - 1, self.item(d, t)).wait_recv()

    def drain(self, d, t):
        self.copy(d, t, self.item(d, t)).wait_send()


STEPS = (8, 7)


def gather_two(yf, yf_own, zf, zf_own, y, z, m, cut_yf, cut_zf, sems):
    yss, yrs, zss, zrs, yss2, yrs2, zss2, zrs2, lsem = sems
    place = (y, z, m)
    a_y = RingY(yf, yss, yrs, cut_yf, place)
    a_z = RingZ(lambda zz: yf.at[:, zz], zss, zrs, place)
    b_y = RingY(zf, yss2, yrs2, cut_zf, place)
    b_z = RingZ(lambda zz: zf.at[y, zz], zss2, zrs2, place)
    locals_ = [
        pltpu.make_async_copy(src, dst, lsem.at[i])
        for i, (src, dst) in enumerate(
            [(src, yf.at[y, z].at[:, cols]) for src, cols in yf_own] + [(zf_own, zf.at[y, z])]
        )
    ]
    for cp in locals_:
        cp.start()
    for cp in locals_:
        cp.wait()
    a_y.start(z)
    b_z.send(0, 0)
    b_z.send(1, 0)
    b_y.start(z)
    a_y.relay(z)
    a_y.finish(z)
    a_z.send(0, 0)
    a_z.send(1, 0)
    b_y.relay(z)

    def step(t, _):
        for d in range(2):
            @pl.when(t <= STEPS[d])
            def _():
                b_z.arrive(d, t)

                @pl.when(t < STEPS[d])
                def _():
                    b_z.send(d, t)

                b_y.start(b_z.item(d, t))
        for d in range(2):
            @pl.when(t <= STEPS[d])
            def _():
                a_z.arrive(d, t)

                @pl.when(t < STEPS[d])
                def _():
                    a_z.send(d, t)
        for d in range(2):
            @pl.when(t <= STEPS[d])
            def _():
                b_y.relay(b_z.item(d, t))
        return 0

    lax.fori_loop(1, 9, step, 0)

    def close(zz, _):
        b_y.finish(zz)
        b_y.drain(zz)
        return 0

    lax.fori_loop(0, NZ, close, 0)
    a_y.drain(z)

    def close_z(t, _):
        for ring in (a_z, b_z):
            for d in range(2):
                @pl.when(t < STEPS[d])
                def _():
                    ring.drain(d, t)
        return 0

    lax.fori_loop(0, 8, close_z, 0)


def gather_sems(n_local):
    return [
        DMA((4, NZ)), DMA((4, NZ)), DMA((2, 8)), DMA((2, 8)),
        DMA((4, NZ)), DMA((4, NZ)), DMA((2, 8)), DMA((2, 8)),
        DMA((n_local,)),
    ]


class MpGather:
    def __init__(self, view, ss, rs, place):
        self.view, self.ss, self.rs = view, ss, rs
        self.s, self.x, self.c = place

    def push(self, k, src=None):
        mine = self.x * NC + self.c
        ref = self.view(mine)
        return pltpu.make_async_remote_copy(
            src_ref=ref if src is None else src, dst_ref=ref, send_sem=self.ss.at[k], recv_sem=self.rs.at[k],
            device_id=(self.s, ((self.x + k) % NX) * NC + self.c), device_id_type=MESH,
        )

    def came(self, k):
        ref = self.view(((self.x + NX - k) % NX) * NC + self.c)
        return pltpu.make_async_remote_copy(
            src_ref=ref, dst_ref=ref, send_sem=self.ss.at[k], recv_sem=self.rs.at[k],
            device_id=(self.s, ((self.x + k) % NX) * NC + self.c), device_id_type=MESH,
        )

    def across(self, k, core):
        ref = self.view(((self.x + NX - k) % NX) * NC + core)
        return pltpu.make_async_remote_copy(
            src_ref=ref, dst_ref=ref, send_sem=self.ss.at[4 + k], recv_sem=self.rs.at[4 + k],
            device_id=(self.s, self.x * NC + 1 - self.c), device_id_type=MESH,
        )

    def start(self):
        for k in (2, 1, 3):
            self.push(k).start()
        self.across(0, self.c).start()

    def relay(self):
        for k in (1, 3, 2):
            self.came(k).wait_recv()
            self.across(k, self.c).start()

    def finish(self):
        for k in (0, 1, 3, 2):
            self.across(k, 1 - self.c).wait_recv()

    def drain(self):
        for k in (1, 2, 3):
            self.push(k).wait_send()
        for k in range(4):
            self.across(k, self.c).wait_send()


def weights_kernel(u_ref, q_ref, k_ref, v_ref, u_out, kv_out, q_out, us, uy, kss, krs, *sems):
    y, z, x, c = coords()
    m = x * NC + c
    enter(yz_peers(y, z, m))
    place = (y, z, m)
    u_y = RingY(u_out, us.at[0], us.at[1], 8, place)
    u_z = RingZ(lambda zz: u_out.at[:, zz], kss, krs, place)
    cp = pltpu.make_async_copy(u_ref, u_out.at[y, z], uy.at[0])
    cp.start()
    cp.wait()
    u_y.start(z)
    u_y.relay(z)
    u_y.finish(z)
    u_z.send(0, 0)
    u_z.send(1, 0)
    gather_two(
        kv_out, [(k_ref, pl.ds(0, HEAD)), (v_ref, pl.ds(HEAD, HEAD))], q_out, q_ref, y, z, m, 32, 32, sems
    )

    def step(t, _):
        for d in range(2):
            @pl.when(t <= STEPS[d])
            def _():
                u_z.arrive(d, t)

                @pl.when(t < STEPS[d])
                def _():
                    u_z.send(d, t)
        return 0

    lax.fori_loop(1, 9, step, 0)
    u_y.drain(z)

    def close_z(t, _):
        for d in range(2):
            @pl.when(t < STEPS[d])
            def _():
                u_z.drain(d, t)
        return 0

    lax.fori_loop(0, 8, close_z, 0)


def params(cid, mib=56):
    return pltpu.CompilerParams(collective_id=cid, has_side_effects=True, vmem_limit_bytes=mib << 20)


def gather_weights(up_weight, query_weight, key_weight, value_weight):
    bf = jnp.bfloat16
    u, kv, q = pl.pallas_call(
        weights_kernel,
        out_shape=[
            jax.ShapeDtypeStruct((NY, NZ, 16, 512), bf),
            jax.ShapeDtypeStruct((NY, NZ, 64, 256), bf),
            jax.ShapeDtypeStruct((NY, NZ, 64, 512), bf),
        ],
        in_specs=[VM] * 4,
        out_specs=[VM] * 3,
        scratch_shapes=[DMA((2, 4, NZ)), DMA((1,)), DMA((2, 8)), DMA((2, 8))] + gather_sems(3),
        compiler_params=params(1),
        name="weights",
    )(up_weight, query_weight, key_weight, value_weight)
    return u.reshape(1024, 512), kv.reshape(4096, 256), q.reshape(4096, 512)


def one_minus_exp(v):
    series = v * (1.0 - v * (0.5 - v * (1 / 6 - v * (1 / 24 - v * (1 / 120 - v / 720)))))
    return jnp.where(v < 0.25, series, 1.0 - jnp.exp(-v))


def scan_rows(decays, drives):
    rows = decays.shape[0]
    ids = lax.broadcasted_iota(jnp.int32, decays.shape, 0)
    k = 1
    while k < rows:
        if k < 8:
            a_back = jnp.where(ids >= k, pltpu.roll(decays, k, 0), 1.0)
            b_back = jnp.where(ids >= k, pltpu.roll(drives, k, 0), 0.0)
        else:
            a_back = jnp.concatenate([jnp.ones((k, decays.shape[1]), jnp.float32), decays[: rows - k]], 0)
            b_back = jnp.concatenate([jnp.zeros((k, decays.shape[1]), jnp.float32), drives[: rows - k]], 0)
        drives = decays * b_back + drives
        decays = decays * a_back
        k *= 2
    return decays, drives


def scan_kernel(
    bytes_ref, gain_ref, win_ref, wstep_ref, rate_ref, mixer_ref,
    states_ref, mixfull_ref,
    pair_ref, line_ref, total_ref, col_ref, pzs, pzr, pys, pyr, gs, gr, ms, mr, lsem,
):
    y, z, x, c = coords()
    s, m = y * NZ + z, x * NC + c
    peers = [(y * NZ + (z + k) % NZ, m) for k in range(1, NZ)]
    peers += [((y + k) % NY * NZ + z, m) for k in range(1, NY)]
    enter(peers + mp_peers(s, x, c))
    mixer = MpGather(lambda mm: mixfull_ref.at[pl.ds(pl.multiple_of(mm * 128, 128), 128)], ms, mr, (s, x, c))
    cp = pltpu.make_async_copy(mixer_ref, mixer.view(m), lsem.at[0])
    cp.start()
    cp.wait()
    mixer.start()

    values = bytes_ref[...].astype(jnp.float32)
    scale = lax.rsqrt(jnp.mean(values * values, axis=-1, keepdims=True) + eps)
    normed = (values * scale * gain_ref[...]).astype(jnp.bfloat16)
    inputs = jnp.dot(normed, win_ref[...], preferred_element_type=jnp.float32)
    raw = jnp.dot(normed, wstep_ref[...], preferred_element_type=jnp.float32)
    small = jnp.exp(-jnp.abs(raw))
    rate = (jnp.maximum(raw, 0.0) + jnp.log1p(small)) * rate_ref[...]
    decays = jnp.exp(-rate)
    drives = jnp.sqrt(one_minus_exp(2.0 * rate)) * inputs
    through, local = scan_rows(decays, drives)
    tile = jnp.concatenate([through[255:256], local[255:256], jnp.zeros((6, 128), jnp.float32)], 0)
    pair_ref[...] = tile
    line_ref[z] = tile

    def zpush(k):
        return remote(pair_ref, line_ref.at[z], pzs.at[k], pzr.at[k], y, (z + k) % NZ, m)

    def zcame(k):
        zz = (z + NZ - k) % NZ
        return remote(pair_ref, line_ref.at[zz], pzs.at[k], pzr.at[k], y, (z + k) % NZ, m)

    def each(f):
        def body(k, _):
            f(k)
            return 0
        lax.fori_loop(1, NZ, body, 0)

    each(lambda k: zpush(k).start())
    mixer.relay()
    each(lambda k: zcame(k).wait_recv())
    zero, one = jnp.zeros((1, 128), jnp.float32), jnp.ones((1, 128), jnp.float32)

    def fold(zz, carry):
        a, b = carry
        pair = line_ref[zz]
        return a * pair[0:1], pair[0:1] * b + pair[1:2]

    before = lax.fori_loop(0, z, fold, (one, zero))
    whole = lax.fori_loop(z, NZ, fold, before)
    tile = jnp.concatenate([whole[0], whole[1], jnp.zeros((6, 128), jnp.float32)], 0)
    total_ref[...] = tile

    def ypush(k):
        return remote(total_ref, col_ref.at[y], pys.at[k], pyr.at[k], (y + k) % NY, z, m)

    def ycame(k):
        return remote(total_ref, col_ref.at[(y + NY - k) % NY], pys.at[k], pyr.at[k], (y + k) % NY, z, m)

    for k in range(1, NY):
        ypush(k).start()
    for k in range(1, NY):
        ycame(k).wait_recv()
    col_ref[y] = tile

    def fold_y(yy, h):
        pair = col_ref[yy]
        return pair[0:1] * h + pair[1:2]

    h = lax.fori_loop(0, y, fold_y, zero)
    arriving = before[0] * h + before[1]
    g = MpGather(lambda mm: states_ref.at[:, pl.ds(pl.multiple_of(mm * 128, 128), 128)], gs, gr, (s, x, c))
    states_ref[:, pl.ds(pl.multiple_of(m * 128, 128), 128)] = (local + through * arriving).astype(jnp.bfloat16)
    g.start()
    g.relay()
    g.finish()
    mixer.finish()
    g.drain()
    mixer.drain()
    each(lambda k: zpush(k).wait_send())
    for k in range(1, NY):
        ypush(k).wait_send()


def scan_stage(byte_states, outer_gain, mamba_input, mamba_step, decay_rate, mixer_weight):
    tile = pltpu.VMEM((8, 128), jnp.float32)
    return pl.pallas_call(
        scan_kernel,
        out_shape=[
            jax.ShapeDtypeStruct((256, 1024), jnp.bfloat16),
            jax.ShapeDtypeStruct((1024, 1024), jnp.bfloat16),
        ],
        in_specs=[VM] * 6,
        out_specs=[VM] * 2,
        scratch_shapes=[
            tile, pltpu.VMEM((NZ, 8, 128), jnp.float32), tile, pltpu.VMEM((NY, 8, 128), jnp.float32),
            DMA((NZ,)), DMA((NZ,)), DMA((NY,)), DMA((NY,)), DMA((8,)), DMA((8,)), DMA((8,)), DMA((8,)), DMA((1,)),
        ],
        compiler_params=params(2),
        name="scan",
    )(byte_states, outer_gain[None, :], mamba_input, mamba_step, decay_rate[None, :], mixer_weight)


def mp_gather_kernel(own_ref, full_ref, ss, rs, lsem):
    y, z, x, c = coords()
    s, m = y * NZ + z, x * NC + c
    width = own_ref.shape[1]
    enter(mp_peers(s, x, c))
    g = MpGather(lambda mm: full_ref.at[:, pl.ds(pl.multiple_of(mm * width, 128), width)], ss, rs, (s, x, c))
    cp = pltpu.make_async_copy(own_ref, g.view(m), lsem.at[0])
    cp.start()
    cp.wait()
    g.start()
    g.relay()
    g.finish()
    g.drain()


def mp_gather(own):
    rows, width = own.shape
    return pl.pallas_call(
        mp_gather_kernel,
        out_shape=jax.ShapeDtypeStruct((rows, width * 8), own.dtype),
        in_specs=[VM],
        out_specs=VM,
        scratch_shapes=[DMA((8,)), DMA((8,)), DMA((1,))],
        compiler_params=params(3),
        name="mp_gather",
    )(own)


def kv_kernel(own_ref, a_out, b_out, *sems):
    y, z, x, c = coords()
    m = x * NC + c
    enter(yz_peers(y, z, m))
    gather_two(
        a_out, [(own_ref.at[pl.ds(0, KV_A)], pl.ds(0, 256))], b_out, own_ref.at[pl.ds(KV_A, CAP - KV_A)],
        y, z, m, 32, 48, sems,
    )


def gather_kv(own):
    return pl.pallas_call(
        kv_kernel,
        out_shape=[
            jax.ShapeDtypeStruct((NY, NZ, KV_A, 256), own.dtype),
            jax.ShapeDtypeStruct((NY, NZ, CAP - KV_A, 256), own.dtype),
        ],
        in_specs=[VM],
        out_specs=[VM] * 2,
        scratch_shapes=gather_sems(2),
        compiler_params=params(4),
        name="kv",
    )(own)


def attend_kernel(q_ref, kva_ref, kvb_ref, ida_ref, idb_ref, rows_ref, out_ref):
    s = lax.axis_index("seq")
    rows = rows_ref[...]
    qs = q_ref[...]
    scale = 1.0 / math.sqrt(HEAD)
    total = qs.shape[0]

    def block(carry, kv, ids):
        peak, denom, acc = carry
        scores = lax.dot_general(qs, kv[:, :HEAD], (((1,), (1,)), ((), ())), preferred_element_type=jnp.float32)
        scores = jnp.where(ids <= rows, scores * scale, masked)
        new_peak = jnp.maximum(peak, jnp.max(scores, axis=1, keepdims=True))
        shrink = jnp.exp(peak - new_peak)
        lifted = jnp.exp(scores - new_peak)
        denom = denom * shrink + jnp.sum(lifted, axis=1, keepdims=True)
        acc = acc * shrink + jnp.dot(lifted.astype(jnp.bfloat16), kv[:, HEAD:], preferred_element_type=jnp.float32)
        return new_peak, denom, acc

    def step(i, carry):
        carry = block(carry, kva_ref[i].reshape(8 * KV_A, 256), ida_ref[i])
        return block(carry, kvb_ref[i].reshape(8 * (CAP - KV_A), 256), idb_ref[i])

    init = (
        jnp.full((total, 1), masked, jnp.float32),
        jnp.zeros((total, 1), jnp.float32),
        jnp.zeros((total, HEAD), jnp.float32),
    )
    _, denom, acc = lax.fori_loop(0, s // 8 + 1, step, init)
    out_ref[...] = (acc / denom).astype(jnp.bfloat16)


def reduce_kernel(part_ref, out_ref, box_ref, ss, rs):
    y, z, x, c = coords()
    s, m = y * NZ + z, x * NC + c
    enter([(s, (m + k) % 8) for k in range(1, 8)])

    def push(k):
        to = (m + k) % 8
        return pltpu.make_async_remote_copy(
            src_ref=part_ref.at[:, pl.ds(pl.multiple_of(to * 128, 128), 128)], dst_ref=box_ref.at[k],
            send_sem=ss.at[k], recv_sem=rs.at[k], device_id=(s, to), device_id_type=MESH,
        )

    for k in range(1, 8):
        push(k).start()
    acc = part_ref[:, pl.ds(pl.multiple_of(m * 128, 128), 128)].astype(jnp.float32)
    for k in range(1, 8):
        push(k).wait_recv()
        acc = acc + box_ref[k].astype(jnp.float32)
    out_ref[...] = acc.astype(jnp.bfloat16)
    for k in range(1, 8):
        push(k).wait_send()


def reduce_mp(part):
    return pl.pallas_call(
        reduce_kernel,
        out_shape=jax.ShapeDtypeStruct((CAP, 128), jnp.bfloat16),
        in_specs=[VM],
        out_specs=VM,
        scratch_shapes=[pltpu.VMEM((8, CAP, 128), jnp.bfloat16), DMA((8,)), DMA((8,))],
        compiler_params=params(5),
        name="reduce_mp",
    )(part)


def on_device(
    byte_states, outer_gain, mamba_input, mamba_step, decay_rate, mixer_weight, boundaries, span_counts,
    up_weight, up_bias, inner_gain, query_weight, key_weight, value_weight, return_weight,
):
    f32, bf = jnp.float32, jnp.bfloat16
    own_shard = lax.axis_index("seq")
    own_lane = lax.axis_index("mp")
    counts = span_counts
    offsets = jnp.cumsum(counts) - counts
    seq_ids = jnp.arange(64, dtype=jnp.int32)
    own_offset = jnp.sum(jnp.where(seq_ids == own_shard, offsets, 0))
    own_count = jnp.sum(jnp.where(seq_ids == own_shard, counts, 0))
    slots = jnp.arange(CAP, dtype=jnp.int32)
    key_ids = jnp.where(slots[None, :] < counts[:, None], offsets[:, None] + slots[None, :], far_index)
    ida = key_ids[:, :KV_A].reshape(8, 1, 8 * KV_A)
    idb = key_ids[:, KV_A:].reshape(8, 1, 8 * (CAP - KV_A))
    query_rows = jnp.tile(own_offset + slots, 4)[:, None]

    u_full, kv_weight, q_weight = gather_weights(up_weight, query_weight, key_weight, value_weight)
    states, mixer = scan_stage(byte_states, outer_gain, mamba_input, mamba_step, decay_rate, mixer_weight)
    mixed = jnp.dot(states, mixer, preferred_element_type=f32)
    encoded = (byte_states.astype(f32) + mixed).astype(bf)
    skip_part = lax.dynamic_slice_in_dim(encoded, own_lane * 128, 128, 1)
    marks = boundaries[0]
    byte_ids = jnp.arange(256, dtype=jnp.int32)
    pick = (jnp.minimum(marks, 255)[:, None] == byte_ids[None, :]).astype(bf)
    pooled = jnp.dot(pick, encoded, preferred_element_type=f32).astype(bf)
    share = (jnp.dot(pooled, u_full, preferred_element_type=f32) + up_bias[None, :]).astype(bf)
    widened = mp_gather(share).astype(f32)
    normed = (
        widened * lax.rsqrt(jnp.mean(widened * widened, axis=-1, keepdims=True) + eps) * inner_gain
    ).astype(bf)
    queries = jnp.dot(normed, q_weight, preferred_element_type=f32).astype(bf)
    kv = jnp.dot(normed, kv_weight, preferred_element_type=f32).astype(bf)
    kva, kvb = gather_kv(kv)
    stacked = queries.reshape(CAP, 4, HEAD).transpose(1, 0, 2).reshape(4 * CAP, HEAD)
    attended = pl.pallas_call(
        attend_kernel,
        out_shape=jax.ShapeDtypeStruct((4 * CAP, HEAD), bf),
        in_specs=[VM] * 6,
        out_specs=VM,
        compiler_params=pltpu.CompilerParams(vmem_limit_bytes=56 << 20),
        name="attend",
    )(stacked, kva.reshape(8, 8, KV_A, 256), kvb.reshape(8, 8, CAP - KV_A, 256), ida, idb, query_rows)
    attended = attended.reshape(4, CAP, HEAD).transpose(1, 0, 2).reshape(CAP, 4 * HEAD)
    projected = jnp.dot(attended, return_weight, preferred_element_type=f32).astype(bf)
    returned = reduce_mp(projected)
    live = slots < own_count
    passed = jnp.sum(((marks[None, :] <= byte_ids[:, None]) & live[None, :]).astype(jnp.int32), axis=1)
    spread = (passed[:, None] - 1 == slots[None, :]).astype(bf)
    back = jnp.dot(spread, returned, preferred_element_type=f32)
    return (skip_part.astype(f32) + back).astype(bf)


def solution(mesh):
    in_specs = (
        P("seq", None), P(), P(None, "mp"), P(None, "mp"), P("mp"), P("mp", None), P("seq", None), P(),
        P("seq", "mp"), P("mp"), P(), P("seq", "mp"), P("seq", "mp"), P("seq", "mp"), P("mp", None),
    )
    return jax.shard_map(on_device, mesh=mesh, in_specs=in_specs, out_specs=P("seq", "mp"), check_vma=False)
```

time: 1140 us -> 252 us (0.22)
  waiting for transfers between devices: 922 us -> 0 us
  Pallas kernels: 0 us -> 227 us
  blocking collectives: 116 us -> 0 us
  matrix products: 41.2 us -> 12.1 us
  other arithmetic: 27.3 us -> 6.71 us
  between operations: 15.9 us -> 0.17 us
    all_gather x7 -> x0, waiting for transfers between devices: 769 us -> none  [the longest x1 140 us: on_device(): key_piece = lax.all_gather(key_rows, 'seq', axis=0, tiled=True)]
    pallas_call x0 -> x6, Pallas kernels: none -> 227 us  [the longest x1 82.1 us: gather_weights(): pl.pallas_call(weights_kernel, out_shape=[jax.ShapeDtypeStruct((NY, NZ, 1...]
    all_gather x2 -> x0, blocking collectives: 116 us -> none  [prefix(): pieces = jax.tree.map(lambda part: lax.all_gather(part, axis), value)]
    psum x1 -> x0, waiting for transfers between devices: 108 us -> none  [on_device(): mixed_sum = lax.psum(partial_value, 'mp')]
    unnamed x10 -> x0, waiting for transfers between devices: 45.3 us -> none
    dot_general x24 -> x6, matrix products: 41.2 us -> 12.1 us  [the longest x1 3.42 us: on_device(): queries = jnp.dot(normed, q_weight, preferred_element_type=f32).astype(bf)]
  transfers between devices with their start and end apart: 9 -> 0, of which waited for: 9 -> 0; matrix products, arithmetic and copies ran while one was open for 1% -> 0% of each run, Pallas kernels for 0% -> 0%
where the time goes in v1:
time: 252 us; the launch traced here: 251 us
  Pallas kernels  227 us (90%)
  matrix products  12.1 us (5%)
  other arithmetic  6.71 us (3%)
  local copies, waits for them, and re-layouts  4.81 us (2%)
    pallas_call x1, Pallas kernels, gather_weights(): pl.pallas_call(weights_kernel, out_shape=[jax.ShapeDtypeStruct((NY, NZ, 1...  82.1 us
    pallas_call x1, Pallas kernels, gather_kv(): pl.pallas_call(kv_kernel, out_shape=[jax.ShapeDtypeStruct((NY, NZ, KV_A,...  46.2 us
    pallas_call x1, Pallas kernels, scan_stage(): pl.pallas_call(scan_kernel, out_shape=[jax.ShapeDtypeStruct((256, 1024),...  40.8 us
    pallas_call x1, Pallas kernels, mp_gather(): pl.pallas_call(mp_gather_kernel, out_shape=jax.ShapeDtypeStruct((rows, wi...  25.7 us
    pallas_call x1, Pallas kernels, reduce_mp(): pl.pallas_call(reduce_kernel, out_shape=jax.ShapeDtypeStruct((CAP, 128),...  17.8 us
    pallas_call x1, Pallas kernels, on_device(): pl.pallas_call(attend_kernel, out_shape=jax.ShapeDtypeStruct((4 * CAP, HE...  14.2 us

profile of v1, /device:TPU:25, one launch (start us, length us, event | category | flops | bytes accessed | tf_op | source)
XLA Modules:
  0.0 250.5 jit_solution(16955257609421264424)
XLA Ops:
  0.0 0.0 copy-start
  0.0 0.7 broadcast_minimum_fusion
  0.7 0.7 copy.24
  1.5 0.1 reduce-window.9
  1.6 0.1 reduce
  1.7 1.4 fusion.16
  3.1 0.6 iota_add_fusion
  3.7 0.7 iota_compare_fusion.7
  4.4 0.8 convert_reduce_fusion
  5.2 0.7 add_select_fusion
  6.0 0.7 reshape.101.ida_ref
  6.7 0.1 slice.9
  6.7 0.7 reshape.98.idb_ref
  7.4 0.9 copy.26.rows_ref
  8.3 40.8 %scan.1 = (bf16[256,1024]{1,0:T(8,128)(2,1)}, bf16[1024,1024]{1,0:T(8,128)(2,1)}) custom-call(bf16[256,1024]{1,0:T(8,128)(2,1)} %bytes_ref.1, f32[1,1024]{1,0:T(1,128)} %bitcast.42, bf16[1024,128]{1,0:T(8,128)(2,1)} %win_ref.1, bf16[1024,128]{1,0:T(8,128)(2,1)} %wstep_ref.1, f32[1,128]{1,0:T(1,128)} %bitcast.43, bf16[128,1024]{1,0:T(8,128)(2,1)} %mixer_ref.1), custom_call_target="tpu_custom_call" | custom-call | tf_op jit(solution)/shard_map/scan/pallas_call | solution.py:445
  49.1 0.0 copy-start.2
  49.1 2.5 %fusion.3 = bf16[256,1024]{1,0:T(8,128)(2,1)S(1)} fusion(bf16[256,1024]{1,0:T(8,128)(2,1)} %get-tuple-element.12, bf16[1024,1024]{1,0:T(8,128)(2,1)} %get-tuple-element.13, bf16[256,1024]{1,0:T(8,128)(2,1)} %bytes_ref.1), kind=kOutput, calls=%fused_computation.6 | convolution fusion | flops 537657344 | bytes 3670016 | tf_op jit(solution)/shard_map/dot_general | solution.py:601
  51.7 0.0 copy-start.4
  51.7 82.1 %weights.1 = (bf16[4,16,16,512]{3,2,1,0:T(8,128)(2,1)}, bf16[4,16,64,256]{3,2,1,0:T(8,128)(2,1)}, bf16[4,16,64,512]{3,2,1,0:T(8,128)(2,1)}) custom-call(bf16[16,512]{1,0:T(8,128)(2,1)} %u_ref.1, bf16[64,512]{1,0:T(8,128)(2,1)} %q_ref.1, bf16[64,128]{1,0:T(8,128)(2,1)} %k_ref.1, bf16[64,128]{1,0:T(8,128)(2,1)} %v_ref.1), custom_call_target="tpu_custom_call" | custom-call | tf_op jit(solution)/shard_map/weights/pallas_call | solution.py:316
  133.7 2.4 fusion.6.own_ref
  136.1 25.7 %mp_gather.1 = bf16[128,4096]{1,0:T(8,128)(2,1)} custom-call(bf16[128,512]{1,0:T(8,128)(2,1)} %fusion.6.own_ref), custom_call_target="tpu_custom_call" | custom-call | tf_op jit(solution)/shard_map/mp_gather/pallas_call | solution.py:479
  161.8 1.5 fusion
  163.4 3.4 %fusion.7 = bf16[16,4,8,128]{3,2,1,0:T(8,128)(2,1)S(1)} fusion(bf16[4096,512]{1,0:T(8,128)(2,1)} %bitcast.45, bf16[128,4096]{1,0:T(8,128)(2,1)} %mp_gather.1, f32[4096]{0:T(1024)S(1)} %copy-done.4, f32[128]{0:T(128)S(1)} %add_rsqrt_fusion), kind=kOutput, calls=%fused_computation.13 | convolution fusion | flops 539033600 | bytes 5390848 | tf_op jit(solution)/shard_map/dot_general | solution.py:613
  166.8 0.0 copy-done.3
  166.8 1.1 convolution_convert_fusion.3.own_ref
  168.0 0.7 copy.30
  168.6 46.2 %kv.1 = (bf16[4,16,48,256]{3,2,1,0:T(8,128)(2,1)}, bf16[4,16,80,256]{3,2,1,0:T(8,128)(2,1)}) custom-call(bf16[128,256]{1,0:T(8,128)(2,1)} %convolution_convert_fusion.3.own_ref), custom_call_target="tpu_custom_call" | custom-call | tf_op jit(solution)/shard_map/kv/pallas_call | solution.py:501
  214.9 14.2 %attend.1 = bf16[512,128]{1,0:T(8,128)(2,1)} custom-call(bf16[512,128]{1,0:T(8,128)(2,1)} %bitcast.36, bf16[8,8,48,256]{3,2,1,0:T(8,128)(2,1)} %bitcast.34, bf16[8,8,80,256]{3,2,1,0:T(8,128)(2,1)} %bitcast.33, s32[8,1,384]{2,1,0:T(1,128)} %reshape.101.ida_ref, s32[8,1,640]{2,1,0:T(1,128)} %reshape.98.idb_ref, s32[512,1]{1,0:T(8,128)} %copy.26.rows_ref), custom_call_target="tpu_custom_call" | custom-call | tf_op jit(solution)/shard_map/attend/pallas_call | solution.py:617
  229.0 1.0 copy.27
  230.1 1.0 convolution_convert_fusion.part_ref
  231.1 17.8 %reduce_mp.1 = bf16[128,128]{1,0:T(8,128)(2,1)} custom-call(bf16[128,1024]{1,0:T(8,128)(2,1)} %convolution_convert_fusion.part_ref), custom_call_target="tpu_custom_call" | custom-call | tf_op jit(solution)/shard_map/reduce_mp/pallas_call | solution.py:570
  248.9 1.6 fusion.8
  (9 shorter events, 0.0 us)
Async XLA Ops:
  0.0 230.1 %copy-start = (bf16[512,1024]{1,0:T(8,128)(2,1)S(1)}, bf16[512,1024]{1,0:T(8,128)(2,1)}, u32[]{:S(2)}) copy-start(bf16[512,1024]{1,0:T(8,128)(2,1)} %param.29) | copy-start | bytes 3145732
  49.1 84.6 %copy-start.2 = (f32[512]{0:T(512)S(1)}, f32[512]{0:T(512)}, u32[]{:S(2)}) copy-start(f32[512]{0:T(512)} %param.24) | copy-start | bytes 6148
  51.7 111.7 %copy-start.4 = (f32[4096]{0:T(1024)S(1)}, f32[4096]{0:T(1024)}, u32[]{:S(2)}) copy-start(f32[4096]{0:T(1024)} %param.25) | copy-start | bytes 49156
  163.3 3.4 %copy-start.1 = (bf16[128,4096]{1,0:T(8,128)(2,1)S(1)}, bf16[128,4096]{1,0:T(8,128)(2,1)}, u32[]{:S(2)}) copy-start(bf16[128,4096]{1,0:T(8,128)(2,1)} %mp_gather.1) | copy-start | bytes 3145732
  163.4 3.5 %copy-start.3 = (bf16[4,16,64,256]{3,2,1,0:T(8,128)(2,1)S(1)}, bf16[4,16,64,256]{3,2,1,0:T(8,128)(2,1)}, u32[]{:S(2)}) copy-start(bf16[4,16,64,256]{3,2,1,0:T(8,128)(2,1)} %get-tuple-element.16) | copy-start | bytes 6291460

commit v2 on v0

v2 whole, which is shorter than its diff:
```python
import math

import jax
import jax.numpy as jnp
from jax import lax
from jax.experimental import pallas as pl
from jax.experimental.pallas import tpu as pltpu
from jax.sharding import PartitionSpec as P

HEADS = 32
KV_HEADS = 8
HEAD = 128
GROUP = HEADS // KV_HEADS
NY, NZ = 4, 16
NX, NC = 4, 2
CAP = 128
ROWS = 256
KV_A = 48
Q_A = 16
STEPS = (8, 7)

eps = 1e-05
masked = -1e30
far_index = 1073741824

MESH = pl.DeviceIdType.MESH
VM = pl.BlockSpec(memory_space=pltpu.VMEM)
SM = pl.BlockSpec(memory_space=pltpu.SMEM)
DMA = pltpu.SemaphoreType.DMA
f32, bf16 = jnp.float32, jnp.bfloat16


def coords():
    s, m = lax.axis_index("seq"), lax.axis_index("mp")
    return s // NZ, s % NZ, m // NC, m % NC


def remote(src, dst, ss, rs, s, m):
    return pltpu.make_async_remote_copy(
        src_ref=src, dst_ref=dst, send_sem=ss, recv_sem=rs, device_id=(s, m), device_id_type=MESH
    )


def when(cond, f):
    if isinstance(cond, bool):
        if cond:
            f()
    else:
        pl.when(cond)(f)


def loop(lo, hi, f):
    def body(i, _):
        f(i)
        return 0

    lax.fori_loop(lo, hi, body, 0)


class PushY:
    def __init__(self, buf, lo, hi, ss, rs, place):
        self.buf, self.lo, self.n, self.ss, self.rs = buf, lo, hi - lo, ss, rs
        self.y, self.z, self.m = place

    def copy(self, k, yy, zz, slot):
        ref = self.buf.at[yy % NY, zz, pl.ds(self.lo, self.n)]
        return remote(ref, ref, self.ss.at[0], self.rs.at[slot], (self.y + k) % NY * NZ + self.z, self.m)

    def start(self, zz, slot):
        for k in (2, 1, 3):
            self.copy(k, self.y, zz, k if slot is None else slot).start()

    def came(self, k):
        self.copy(k, self.y + NY - k, self.z, k).wait_recv()

    def wait(self, columns, slot=0):
        ref = self.buf.at[pl.ds(0, 3), pl.ds(0, columns), pl.ds(self.lo, self.n)]
        pltpu.make_async_copy(ref, ref, self.rs.at[slot]).wait()

    def drain(self, columns):
        ref = self.buf.at[pl.ds(0, 3), pl.ds(0, columns), pl.ds(self.lo, self.n)]
        pltpu.make_async_copy(ref, ref, self.ss.at[0]).wait()


class RingZ:
    def __init__(self, buf, lo, hi, k, ss, rs, place):
        self.buf, self.lo, self.n, self.k, self.ss, self.rs = buf, lo, hi - lo, k, ss, rs
        self.y, self.z, self.m = place

    def item(self, d, t):
        return (self.z + (NZ - t if d == 0 else t)) % NZ

    def copy(self, d, t, zz):
        ref = self.buf.at[(self.y + self.k) % NY, zz, pl.ds(self.lo, self.n)]
        to = (self.z + (1 if d == 0 else NZ - 1)) % NZ
        return remote(ref, ref, self.ss.at[0], self.rs.at[2 * self.k + d, t], self.y * NZ + to, self.m)

    def own(self):
        for d in range(2):
            self.copy(d, 0, self.z).start()

    def step(self, d, t):
        zz = self.item(d, t)
        self.copy(d, t - 1, zz).wait_recv()
        when(t < STEPS[d], lambda: self.copy(d, t, zz).start())

    def drain(self, blocks):
        ref = self.buf.at[pl.ds(0, blocks), pl.ds(0, NZ - 1), pl.ds(self.lo, self.n)]
        pltpu.make_async_copy(ref, ref, self.ss.at[0]).wait()


class YFirst:
    def __init__(self, buf, lo, hi, sems, place):
        yss, yrs, zss, zrs = sems
        self.z = place[1]
        self.push = PushY(buf, lo, hi, yss, yrs, place)
        self.rings = [RingZ(buf, lo, hi, k, zss, zrs, place) for k in range(NY)]

    def own(self):
        self.push.start(self.z, None)
        self.rings[0].own()

    def spread(self):
        for k in (1, 3, 2):
            self.push.came(k)
            self.rings[NY - k].own()

    def step(self, t):
        for d in range(2):
            def go():
                for k in (0, 3, 1, 2):
                    self.rings[k].step(d, t)
            when(t <= STEPS[d], go)

    def drain(self):
        self.push.drain(1)
        self.rings[0].drain(NY)


class ZFirst:
    def __init__(self, buf, lo, hi, sems, place, by_column=False):
        yss, yrs, zss, zrs = sems
        self.z, self.by_column = place[1], by_column
        self.push = PushY(buf, lo, hi, yss, yrs, place)
        self.ring = RingZ(buf, lo, hi, 0, zss, zrs, place)

    def start(self, zz):
        self.push.start(zz, zz if self.by_column else 0)

    def own(self):
        self.ring.own()
        self.start(self.z)

    def step(self, t):
        for d in range(2):
            def go():
                self.ring.step(d, t)
                self.start(self.ring.item(d, t))
            when(t <= STEPS[d], go)

    def finish(self):
        self.push.wait(NZ)

    def drain(self):
        self.push.drain(NZ)
        self.ring.drain(1)


def ring_sems(y_first):
    zs = (8, 8) if y_first else (2, 8)
    return [DMA((1,)), DMA((NZ,)), DMA((1,)), DMA(zs)]


class MpGather:
    def __init__(self, view, ss, rs, place):
        self.view, self.ss, self.rs = view, ss, rs
        self.s, self.x, self.c = place

    def same(self, k, back):
        ref = self.view(((self.x + (NX - k if back else 0)) % NX) * NC + self.c)
        return remote(ref, ref, self.ss.at[k], self.rs.at[k], self.s, ((self.x + k) % NX) * NC + self.c)

    def across(self, k, core):
        ref = self.view(((self.x + NX - k) % NX) * NC + core)
        return remote(ref, ref, self.ss.at[4 + k], self.rs.at[4 + k], self.s, self.x * NC + 1 - self.c)

    def start(self):
        for k in (2, 1, 3):
            self.same(k, False).start()
        self.across(0, self.c).start()

    def relay(self):
        for k in (1, 3, 2):
            self.same(k, True).wait_recv()
            self.across(k, self.c).start()

    def finish(self):
        for k in (0, 1, 3, 2):
            self.across(k, 1 - self.c).wait_recv()

    def drain(self):
        for k in (1, 2, 3):
            self.same(k, False).wait_send()
        for k in range(4):
            self.across(k, self.c).wait_send()


def one_minus_exp(v):
    series = v * (1.0 - v * (0.5 - v * (1 / 6 - v * (1 / 24 - v * (1 / 120 - v / 720)))))
    return jnp.where(v < 0.25, series, 1.0 - jnp.exp(-v))


def scan_rows(decays, drives):
    rows = decays.shape[0]
    ids = lax.broadcasted_iota(jnp.int32, decays.shape, 0)
    k = 1
    while k < rows:
        if k < 8:
            a_back = jnp.where(ids >= k, pltpu.roll(decays, k, 0), 1.0)
            b_back = jnp.where(ids >= k, pltpu.roll(drives, k, 0), 0.0)
        else:
            a_back = jnp.concatenate([jnp.ones((k, decays.shape[1]), f32), decays[: rows - k]], 0)
            b_back = jnp.concatenate([jnp.zeros((k, decays.shape[1]), f32), drives[: rows - k]], 0)
        drives = decays * b_back + drives
        decays = decays * a_back
        k *= 2
    return decays, drives


def block_cols(m, width=128):
    return pl.ds(pl.multiple_of(m * width, 128), width)


def row_of(ref):
    return ref[...].reshape(1, ref.shape[0])


def kernel(
    counts_ref, marks_ref, gain_ref, rate_ref, bias_ref, igain_ref,
    bytes_hbm, win_hbm, wstep_hbm, mixer_hbm, up_hbm, wq_hbm, wk_hbm, wv_hbm, wret_hbm,
    out_ref,
    offs_ref, bytes_ref, win_ref, wstep_ref, wret_ref, through_ref, local_ref, pair_ref, line_ref, total_ref, col_ref,
    states_ref, mix_ref, u_ref, kvw_ref, q_ref, kv_ref, stage_ref, enc_ref, wide_ref, peak_ref, denom_ref, acc_ref,
    part_ref, box_ref,
    pzs, pzr, pys, pyr, gs, gr, ms, mr, ws, wr, bs, br, lsem, *ring,
):
    y, z, x, c = coords()
    s, m = y * NZ + z, x * NC + c
    place = (y, z, m)
    peers = [(y * NZ + (z + k) % NZ, m) for k in range(1, NZ)]
    peers += [((y + k) % NY * NZ + z, m) for k in range(1, NY)]
    peers += [(s, (m + k) % 8) for k in range(1, 8)]
    barrier = pltpu.get_barrier_semaphore()
    for seq, mp in peers:
        pl.semaphore_signal(barrier, inc=1, device_id=(seq, mp), device_id_type=MESH)

    u = YFirst(u_ref, 0, 16, ring[0:4], place)
    kvw = ZFirst(kvw_ref, 0, 64, ring[4:8], place)
    qa = YFirst(q_ref, 0, Q_A, ring[8:12], place)
    qb = ZFirst(q_ref, Q_A, 64, ring[12:16], place)
    kva = YFirst(kv_ref, 0, KV_A, ring[16:20], place)
    kvb = ZFirst(kv_ref, KV_A, CAP, ring[20:24], place, by_column=True)
    mixer = MpGather(lambda mm: mix_ref.at[pl.ds(pl.multiple_of(mm * 128, 128), 128)], ms, mr, (s, x, c))
    g = MpGather(lambda mm: states_ref.at[:, block_cols(mm)], gs, gr, (s, x, c))
    w = MpGather(lambda mm: wide_ref.at[:, block_cols(mm, 512)], ws, wr, (s, x, c))

    copies = [
        pltpu.make_async_copy(src, dst, lsem.at[i])
        for i, (src, dst) in enumerate([
            (bytes_hbm, bytes_ref),
            (win_hbm, win_ref),
            (wstep_hbm, wstep_ref),
            (up_hbm, u_ref.at[y, z]),
            (wk_hbm, kvw_ref.at[y, z, :, pl.ds(0, HEAD)]),
            (wv_hbm, kvw_ref.at[y, z, :, pl.ds(HEAD, HEAD)]),
            (wq_hbm, q_ref.at[y, z]),
            (mixer_hbm, mixer.view(m)),
            (wret_hbm, wret_ref),
        ])
    ]
    for cp in copies:
        cp.start()

    def offsets(i, acc):
        offs_ref[i] = acc
        return acc + counts_ref[i]

    lax.fori_loop(0, 64, offsets, jnp.int32(0))
    for cp in copies[:3]:
        cp.wait()

    values = bytes_ref[...].astype(f32)
    scale = lax.rsqrt(jnp.mean(values * values, axis=-1, keepdims=True) + eps)
    normed = (values * scale * row_of(gain_ref)).astype(bf16)
    inputs = jnp.dot(normed, win_ref[...], preferred_element_type=f32)
    raw = jnp.dot(normed, wstep_ref[...], preferred_element_type=f32)
    rate = (jnp.maximum(raw, 0.0) + jnp.log1p(jnp.exp(-jnp.abs(raw)))) * row_of(rate_ref)
    through, local = scan_rows(jnp.exp(-rate), jnp.sqrt(one_minus_exp(2.0 * rate)) * inputs)
    through_ref[...] = through
    local_ref[...] = local
    tile = jnp.concatenate([through[ROWS - 1 :], local[ROWS - 1 :], jnp.zeros((6, 128), f32)], 0)
    pair_ref[...] = tile
    line_ref[z] = tile
    for cp in copies[3:]:
        cp.wait()
    pl.semaphore_wait(barrier, len(peers))

    def zpush(k):
        return remote(pair_ref, line_ref.at[z], pzs.at[k], pzr.at[k], y * NZ + (z + k) % NZ, m)

    def zcame(k):
        ref = line_ref.at[(z + NZ - k) % NZ]
        return remote(ref, ref, pzs.at[k], pzr.at[k], y * NZ + (z + k) % NZ, m)

    def ypush(k):
        return remote(total_ref, col_ref.at[y], pys.at[k], pyr.at[k], (y + k) % NY * NZ + z, m)

    def ycame(k):
        ref = col_ref.at[(y + NY - k) % NY]
        return remote(ref, ref, pys.at[k], pyr.at[k], (y + k) % NY * NZ + z, m)

    def step_a(t):
        u.step(t)
        kvw.step(t)

    def step_q(t):
        qa.step(t)
        qb.step(t)

    loop(1, NZ, lambda k: zpush(k).start())
    u.own()
    kvw.own()
    qa.own()
    qb.own()
    mixer.start()
    u.spread()
    qa.spread()
    loop(1, 3, step_a)
    step_q(1)
    loop(1, NZ, lambda k: zcame(k).wait_recv())
    zero, one = jnp.zeros((1, 128), f32), jnp.ones((1, 128), f32)

    def fold(zz, carry):
        pair = line_ref[zz]
        return carry[0] * pair[0:1], pair[0:1] * carry[1] + pair[1:2]

    before = lax.fori_loop(0, z, fold, (one, zero))
    whole = lax.fori_loop(z, NZ, fold, before)
    tile = jnp.concatenate([whole[0], whole[1], jnp.zeros((6, 128), f32)], 0)
    total_ref[...] = tile
    col_ref[y] = tile
    for k in range(1, NY):
        ypush(k).start()
    step_a(3)
    for k in range(1, NY):
        ycame(k).wait_recv()

    def fold_y(yy, h):
        pair = col_ref[yy]
        return pair[0:1] * h + pair[1:2]

    arriving = before[0] * lax.fori_loop(0, y, fold_y, zero) + before[1]
    states_ref[:, block_cols(m)] = (local_ref[...] + through_ref[...] * arriving).astype(bf16)
    g.start()
    mixer.relay()
    step_a(4)
    g.relay()
    step_a(5)
    g.finish()
    mixer.finish()
    step_q(2)

    mixed = jnp.dot(states_ref[...], mix_ref[...], preferred_element_type=f32)
    enc_ref[...] = (bytes_ref[...].astype(f32) + mixed).astype(bf16)
    step_a(6)
    marks = marks_ref[...]
    byte_ids = lax.broadcasted_iota(jnp.int32, (ROWS, CAP), 0)
    pick = jnp.where(jnp.minimum(marks, ROWS - 1) == byte_ids, 1.0, 0.0).astype(bf16)
    pooled = lax.dot_general(
        pick, enc_ref[...], (((0,), (0,)), ((), ())), preferred_element_type=f32
    ).astype(bf16)
    loop(7, 9, step_a)
    u_full = u_ref[...].reshape(1024, 512)
    share = jnp.dot(pooled, u_full, preferred_element_type=f32) + row_of(bias_ref)
    wide_ref[:, block_cols(m, 512)] = share.astype(bf16)
    w.start()
    loop(3, 5, step_q)
    w.relay()
    step_q(5)
    w.finish()
    wide = wide_ref[...].astype(f32)
    scale = lax.rsqrt(jnp.mean(wide * wide, axis=-1, keepdims=True) + eps)
    wide_n = (wide * scale * row_of(igain_ref)).astype(bf16)
    kvw.finish()
    kv = jnp.dot(wide_n, kvw_ref[...].reshape(4096, 256), preferred_element_type=f32)
    kv_ref[y, z] = kv.astype(bf16)
    kva.own()
    kvb.own()
    step_q(6)
    kva.spread()

    def step_kv(t):
        kva.step(t)
        kvb.step(t)

    def step_both(t):
        step_q(t + 6)
        step_kv(t)

    loop(1, 3, step_both)
    qb.finish()
    queries = jnp.dot(wide_n, q_ref[...].reshape(4096, 512), preferred_element_type=f32).astype(bf16)
    stacked = jnp.concatenate([queries[:, h * HEAD : (h + 1) * HEAD] for h in range(GROUP)], 0)

    total = GROUP * CAP
    own_rows = offs_ref[s] + (lax.broadcasted_iota(jnp.int32, (total, 1), 0) & (CAP - 1))
    slots = lax.broadcasted_iota(jnp.int32, (1, CAP), 1)
    peak_ref[...] = jnp.full((total, CAP), masked, f32)
    denom_ref[...] = jnp.zeros((total, CAP), f32)
    acc_ref[...] = jnp.zeros((total, HEAD), f32)

    def ids_of(zz):
        return [
            jnp.where(slots < counts_ref[yy * NZ + zz], offs_ref[yy * NZ + zz] + slots, far_index)
            for yy in range(NY)
        ]

    def turn(j):
        pl.when(j <= 5)(lambda: step_kv(j + 3))
        columns = ((z + j) % NZ, (z + NZ - 1 - j) % NZ)
        staged = []
        for i, zz in enumerate(columns):
            kvb.push.wait(1, zz)
            staged.append(pltpu.make_async_copy(kv_ref.at[:, zz], stage_ref.at[i], lsem.at[i]))
            staged[i].start()
        ids = jnp.concatenate(ids_of(columns[0]) + ids_of(columns[1]), 1)
        for cp in staged:
            cp.wait()
        kv = stage_ref[...].reshape(2 * NY * CAP, 2 * HEAD)
        scores = lax.dot_general(stacked, kv[:, :HEAD], (((1,), (1,)), ((), ())), preferred_element_type=f32)
        scores = jnp.where(ids <= own_rows, scores * (1.0 / math.sqrt(HEAD)), masked)
        peak = peak_ref[:, 0:1]
        new_peak = jnp.maximum(peak, jnp.max(scores, axis=1, keepdims=True))
        shrink = jnp.exp(peak - new_peak)
        lifted = jnp.exp(scores - new_peak)
        denom = denom_ref[:, 0:1] * shrink + jnp.sum(lifted, axis=1, keepdims=True)
        acc = jnp.dot(lifted.astype(bf16), kv[:, HEAD:], preferred_element_type=f32)
        acc_ref[...] = acc_ref[...] * shrink + acc
        peak_ref[...] = jnp.broadcast_to(new_peak, (total, CAP))
        denom_ref[...] = jnp.broadcast_to(denom, (total, CAP))

    loop(0, 8, turn)
    attended = (acc_ref[...] / denom_ref[...]).astype(bf16)
    attended = jnp.concatenate([attended[h * CAP : (h + 1) * CAP] for h in range(GROUP)], 1)

    part_ref[...] = jnp.dot(attended, wret_ref[...], preferred_element_type=f32).astype(bf16)

    def push(k):
        to = (m + k) % 8
        return remote(part_ref.at[:, block_cols(to)], box_ref.at[k], bs.at[k], br.at[k], s, to)

    for k in range(1, 8):
        push(k).start()
    live = (marks <= byte_ids) & (lax.broadcasted_iota(jnp.int32, (ROWS, CAP), 1) < counts_ref[s])
    passed = jnp.sum(jnp.where(live, 1.0, 0.0), axis=1, keepdims=True)
    lane = lax.broadcasted_iota(jnp.int32, (ROWS, CAP), 1).astype(f32)
    spread = jnp.where(passed - 1.0 == lane, 1.0, 0.0).astype(bf16)

    for gather in (mixer, g, w):
        gather.drain()
    loop(1, NZ, lambda k: zpush(k).wait_send())
    for k in range(1, NY):
        ypush(k).wait_send()
    for stream in (u, kvw, qa, qb, kva, kvb):
        stream.drain()

    acc = part_ref[:, block_cols(m)].astype(f32)
    for k in range(1, 8):
        push(k).wait_recv()
        acc = acc + box_ref[k].astype(f32)
    back = jnp.dot(spread, acc.astype(bf16), preferred_element_type=f32)
    out_ref[...] = (enc_ref[:, block_cols(m)].astype(f32) + back).astype(bf16)
    for k in range(1, 8):
        push(k).wait_send()


def on_device(
    byte_states, outer_gain, mamba_input, mamba_step, decay_rate, mixer_weight, boundaries, span_counts,
    up_weight, up_bias, inner_gain, query_weight, key_weight, value_weight, return_weight,
):
    tile = pltpu.VMEM((8, 128), f32)
    rings = []
    for y_first in (True, False, True, False, True, False):
        rings += ring_sems(y_first)
    return pl.pallas_call(
        kernel,
        out_shape=jax.ShapeDtypeStruct((ROWS, 128), bf16),
        in_specs=[SM] + [VM] * 5 + [pl.BlockSpec(memory_space=pl.ANY)] * 9,
        out_specs=VM,
        scratch_shapes=[
            pltpu.SMEM((64,), jnp.int32),
            pltpu.VMEM((ROWS, 1024), bf16), pltpu.VMEM((1024, 128), bf16), pltpu.VMEM((1024, 128), bf16),
            pltpu.VMEM((512, 1024), bf16),
            pltpu.VMEM((ROWS, 128), f32), pltpu.VMEM((ROWS, 128), f32),
            tile, pltpu.VMEM((NZ, 8, 128), f32), tile, pltpu.VMEM((NY, 8, 128), f32),
            pltpu.VMEM((ROWS, 1024), bf16), pltpu.VMEM((1024, 1024), bf16),
            pltpu.VMEM((NY, NZ, 16, 512), bf16), pltpu.VMEM((NY, NZ, 64, 256), bf16),
            pltpu.VMEM((NY, NZ, 64, 512), bf16), pltpu.VMEM((NY, NZ, CAP, 256), bf16),
            pltpu.VMEM((2, NY, CAP, 256), bf16),
            pltpu.VMEM((ROWS, 1024), bf16), pltpu.VMEM((CAP, 4096), bf16),
            pltpu.VMEM((GROUP * CAP, CAP), f32), pltpu.VMEM((GROUP * CAP, CAP), f32),
            pltpu.VMEM((GROUP * CAP, HEAD), f32),
            pltpu.VMEM((CAP, 1024), bf16), pltpu.VMEM((8, CAP, 128), bf16),
            DMA((NZ,)), DMA((NZ,)), DMA((NY,)), DMA((NY,)),
            DMA((8,)), DMA((8,)), DMA((8,)), DMA((8,)), DMA((8,)), DMA((8,)), DMA((8,)), DMA((8,)),
            DMA((9,)),
        ] + rings,
        compiler_params=pltpu.CompilerParams(collective_id=1, has_side_effects=True, vmem_limit_bytes=58 << 20),
        name="window",
    )(
        span_counts, boundaries, outer_gain, decay_rate, up_bias, inner_gain,
        byte_states, mamba_input, mamba_step, mixer_weight,
        up_weight, query_weight, key_weight, value_weight, return_weight,
    )


def solution(mesh):
    in_specs = (
        P("seq", None), P(), P(None, "mp"), P(None, "mp"), P("mp"), P("mp", None), P("seq", None), P(),
        P("seq", "mp"), P("mp"), P(), P("seq", "mp"), P("seq", "mp"), P("seq", "mp"), P("mp", None),
    )
    return jax.shard_map(on_device, mesh=mesh, in_specs=in_specs, out_specs=P("seq", "mp"), check_vma=False)
```

time: 1140 us -> 131 us (0.11)
  waiting for transfers between devices: 922 us -> 0 us
  Pallas kernels: 0 us -> 128 us
  blocking collectives: 116 us -> 0 us
  matrix products: 41.2 us -> 0 us
  other arithmetic: 27.3 us -> 0 us
  between operations: 15.9 us -> 0.01 us
    all_gather x7 -> x0, waiting for transfers between devices: 769 us -> none  [the longest x1 140 us: on_device(): key_piece = lax.all_gather(key_rows, 'seq', axis=0, tiled=True)]
    pallas_call x0 -> x1, Pallas kernels: none -> 128 us  [on_device(): pl.pallas_call(kernel, out_shape=jax.ShapeDtypeStruct((ROWS, 128), bf16),...]
    all_gather x2 -> x0, blocking collectives: 116 us -> none  [prefix(): pieces = jax.tree.map(lambda part: lax.all_gather(part, axis), value)]
    psum x1 -> x0, waiting for transfers between devices: 108 us -> none  [on_device(): mixed_sum = lax.psum(partial_value, 'mp')]
    unnamed x10 -> x0, waiting for transfers between devices: 45.3 us -> none
    dot_general x24 -> x0, matrix products: 41.2 us -> none  [the longest x8 15.9 us: attend_block(): jnp.einsum('hqd,khd->hqk', grouped, key_block, preferred_element_type=jnp...]
    reduce_sum x20 -> x0, other arithmetic: 14.1 us -> none  [the longest x8 6.28 us: pick_table(): jnp.sum(jnp.where(seq_ids[None, :] == wanted[:, None], table[None, :], 0)...]
  transfers between devices with their start and end apart: 9 -> 0, of which waited for: 9 -> 0; matrix products, arithmetic and copies ran while one was open for 1% -> 0% of each run, Pallas kernels for 0% -> 0%
where the time goes in v2:
time: 131 us; the launch traced here: 129 us
  Pallas kernels  128 us (98%)
  local copies, waits for them, and re-layouts  1.47 us (1%)
    pallas_call x1, Pallas kernels, on_device(): pl.pallas_call(kernel, out_shape=jax.ShapeDtypeStruct((ROWS, 128), bf16),...  128 us

profile of v2, /device:TPU:25, one launch (start us, length us, event | category | flops | bytes accessed | tf_op | source)
XLA Modules:
  0.0 129.3 jit_solution(2755257052177789199)
XLA Ops:
  0.0 127.9 %window.1 = bf16[256,128]{1,0:T(8,128)(2,1)} custom-call(s32[64]{0:T(128)} %counts_ref.1, s32[1,128]{1,0:T(1,128)} %marks_ref.1, f32[1024]{0:T(1024)} %gain_ref.1, f32[128]{0:T(128)} %rate_ref.1, f32[512]{0:T(512)} %bias_ref.1, f32[4096]{0:T(1024)} %igain_ref.1, bf16[256,1024]{1,0:T(8,128)(2,1)} %bytes_hbm.1, bf16[1024,128]{1,0:T(8,128)(2,1)} %win_hbm.1, ...), custom_call_target="tpu_custom_call" | custom-call | tf_op jit(solution)/shard_map/window/pallas_call | solution.py:495
  127.9 1.5 %copy.17 = bf16[256,128]{1,0:T(8,128)(2,1)} copy(bf16[256,128]{1,0:T(8,128)(2,1)} %window.1) | data formatting | bytes 131072

commit v3 on v2

--- a/solution.py
+++ b/solution.py
@@ -15,8 +15,8 @@
 NX, NC = 4, 2
 CAP = 128
 ROWS = 256
-KV_A = 48
-Q_A = 16
+KV_A = 32
+Q_A = 32
 STEPS = (8, 7)
 
 eps = 1e-05

time: 131 us -> 126 us (0.962)
  Pallas kernels: 128 us -> 122 us
    pallas_call x1, Pallas kernels: 128 us -> 122 us  [on_device(): pl.pallas_call(kernel, out_shape=jax.ShapeDtypeStruct((ROWS, 128), bf16),...]
where the time goes in v3:
time: 126 us; the launch traced here: 124 us
  Pallas kernels  122 us (97%)
  local copies, waits for them, and re-layouts  1.47 us (1%)
    pallas_call x1, Pallas kernels, on_device(): pl.pallas_call(kernel, out_shape=jax.ShapeDtypeStruct((ROWS, 128), bf16),...  122 us

profile of v3, /device:TPU:25, one launch (start us, length us, event | category | flops | bytes accessed | tf_op | source)
XLA Modules:
  0.0 123.7 jit_solution(4999076337375337844)
XLA Ops:
  0.0 122.2 %window.1 = bf16[256,128]{1,0:T(8,128)(2,1)} custom-call(s32[64]{0:T(128)} %counts_ref.1, s32[1,128]{1,0:T(1,128)} %marks_ref.1, f32[1024]{0:T(1024)} %gain_ref.1, f32[128]{0:T(128)} %rate_ref.1, f32[512]{0:T(512)} %bias_ref.1, f32[4096]{0:T(1024)} %igain_ref.1, bf16[256,1024]{1,0:T(8,128)(2,1)} %bytes_hbm.1, bf16[1024,128]{1,0:T(8,128)(2,1)} %win_hbm.1, ...), custom_call_target="tpu_custom_call" | custom-call | tf_op jit(solution)/shard_map/window/pallas_call | solution.py:495
  122.2 1.5 %copy.17 = bf16[256,128]{1,0:T(8,128)(2,1)} copy(bf16[256,128]{1,0:T(8,128)(2,1)} %window.1) | data formatting | bytes 131072

commit v4 on v3

--- a/solution.py
+++ b/solution.py
@@ -58,9 +58,15 @@
 
 
 class PushY:
-    def __init__(self, buf, lo, hi, ss, rs, place):
-        self.buf, self.lo, self.n, self.ss, self.rs = buf, lo, hi - lo, ss, rs
+    def __init__(self, buf, lo, hi, ss, rs, place, causal=False):
+        self.buf, self.lo, self.n, self.ss, self.rs, self.causal = buf, lo, hi - lo, ss, rs, causal
         self.y, self.z, self.m = place
+
+    def to(self, k):
+        return self.y + k < NY if self.causal else True
+
+    def of(self, k):
+        return self.y >= k if self.causal else True
 
     def copy(self, k, yy, zz, slot):
         ref = self.buf.at[yy % NY, zz, pl.ds(self.lo, self.n)]
@@ -68,16 +74,28 @@
 
     def start(self, zz, slot):
         for k in (2, 1, 3):
-            self.copy(k, self.y, zz, k if slot is None else slot).start()
+            when(self.to(k), lambda: self.copy(k, self.y, zz, k if slot is None else slot).start())
 
     def came(self, k):
         self.copy(k, self.y + NY - k, self.z, k).wait_recv()
 
     def wait(self, columns, slot=0):
+        if self.causal:
+            pl.when(self.y > 0)(lambda: self.take(self.rs.at[slot], columns))
+            return
         ref = self.buf.at[pl.ds(0, 3), pl.ds(0, columns), pl.ds(self.lo, self.n)]
         pltpu.make_async_copy(ref, ref, self.rs.at[slot]).wait()
 
+    def take(self, sem, columns, sent=False):
+        for n in range(1, NY):
+            ref = self.buf.at[pl.ds(0, n), pl.ds(0, columns), pl.ds(self.lo, self.n)]
+            have = self.y == (NY - 1 - n if sent else n)
+            pl.when(have)(lambda: pltpu.make_async_copy(ref, ref, sem).wait())
+
     def drain(self, columns):
+        if self.causal:
+            self.take(self.ss.at[0], columns, True)
+            return
         ref = self.buf.at[pl.ds(0, 3), pl.ds(0, columns), pl.ds(self.lo, self.n)]
         pltpu.make_async_copy(ref, ref, self.ss.at[0]).wait()
 
@@ -110,10 +128,10 @@
 
 
 class YFirst:
-    def __init__(self, buf, lo, hi, sems, place):
+    def __init__(self, buf, lo, hi, sems, place, causal=False):
         yss, yrs, zss, zrs = sems
-        self.z = place[1]
-        self.push = PushY(buf, lo, hi, yss, yrs, place)
+        self.y, self.z, self.causal = place[0], place[1], causal
+        self.push = PushY(buf, lo, hi, yss, yrs, place, causal)
         self.rings = [RingZ(buf, lo, hi, k, zss, zrs, place) for k in range(NY)]
 
     def own(self):
@@ -122,26 +140,32 @@
 
     def spread(self):
         for k in (1, 3, 2):
-            self.push.came(k)
-            self.rings[NY - k].own()
+            def go():
+                self.push.came(k)
+                self.rings[NY - k].own()
+            when(self.push.of(k), go)
 
     def step(self, t):
         for d in range(2):
             def go():
                 for k in (0, 3, 1, 2):
-                    self.rings[k].step(d, t)
+                    when(self.push.of(NY - k) if k else True, lambda: self.rings[k].step(d, t))
             when(t <= STEPS[d], go)
 
     def drain(self):
         self.push.drain(1)
-        self.rings[0].drain(NY)
+        if self.causal:
+            for n in range(1, NY + 1):
+                pl.when(self.y == n - 1)(lambda: self.rings[0].drain(n))
+        else:
+            self.rings[0].drain(NY)
 
 
 class ZFirst:
     def __init__(self, buf, lo, hi, sems, place, by_column=False):
         yss, yrs, zss, zrs = sems
         self.z, self.by_column = place[1], by_column
-        self.push = PushY(buf, lo, hi, yss, yrs, place)
+        self.push = PushY(buf, lo, hi, yss, yrs, place, by_column)
         self.ring = RingZ(buf, lo, hi, 0, zss, zrs, place)
 
     def start(self, zz):
@@ -258,7 +282,7 @@
     kvw = ZFirst(kvw_ref, 0, 64, ring[4:8], place)
     qa = YFirst(q_ref, 0, Q_A, ring[8:12], place)
     qb = ZFirst(q_ref, Q_A, 64, ring[12:16], place)
-    kva = YFirst(kv_ref, 0, KV_A, ring[16:20], place)
+    kva = YFirst(kv_ref, 0, KV_A, ring[16:20], place, causal=True)
     kvb = ZFirst(kv_ref, KV_A, CAP, ring[20:24], place, by_column=True)
     mixer = MpGather(lambda mm: mix_ref.at[pl.ds(pl.multiple_of(mm * 128, 128), 128)], ms, mr, (s, x, c))
     g = MpGather(lambda mm: states_ref.at[:, block_cols(mm)], gs, gr, (s, x, c))
@@ -303,6 +327,11 @@
     line_ref[z] = tile
     for cp in copies[3:]:
         cp.wait()
+
+    def clear(yy):
+        kv_ref[yy] = jnp.zeros((NZ, CAP, 2 * HEAD), bf16)
+
+    loop(y + 1, NY, clear)
     pl.semaphore_wait(barrier, len(peers))
 
     def zpush(k):
@@ -335,8 +364,7 @@
     mixer.start()
     u.spread()
     qa.spread()
-    loop(1, 3, step_a)
-    step_q(1)
+    step_a(1)
     loop(1, NZ, lambda k: zcame(k).wait_recv())
     zero, one = jnp.zeros((1, 128), f32), jnp.ones((1, 128), f32)
 
@@ -351,7 +379,8 @@
     col_ref[y] = tile
     for k in range(1, NY):
         ypush(k).start()
-    step_a(3)
+    step_a(2)
+    step_q(1)
     for k in range(1, NY):
         ycame(k).wait_recv()
 
@@ -363,30 +392,33 @@
     states_ref[:, block_cols(m)] = (local_ref[...] + through_ref[...] * arriving).astype(bf16)
     g.start()
     mixer.relay()
+    step_a(3)
+    step_q(2)
+    g.relay()
     step_a(4)
-    g.relay()
-    step_a(5)
     g.finish()
     mixer.finish()
-    step_q(2)
+    step_q(3)
 
     mixed = jnp.dot(states_ref[...], mix_ref[...], preferred_element_type=f32)
     enc_ref[...] = (bytes_ref[...].astype(f32) + mixed).astype(bf16)
-    step_a(6)
+    step_a(5)
     marks = marks_ref[...]
     byte_ids = lax.broadcasted_iota(jnp.int32, (ROWS, CAP), 0)
     pick = jnp.where(jnp.minimum(marks, ROWS - 1) == byte_ids, 1.0, 0.0).astype(bf16)
     pooled = lax.dot_general(
         pick, enc_ref[...], (((0,), (0,)), ((), ())), preferred_element_type=f32
     ).astype(bf16)
+    step_a(6)
+    step_q(4)
     loop(7, 9, step_a)
     u_full = u_ref[...].reshape(1024, 512)
     share = jnp.dot(pooled, u_full, preferred_element_type=f32) + row_of(bias_ref)
     wide_ref[:, block_cols(m, 512)] = share.astype(bf16)
     w.start()
-    loop(3, 5, step_q)
+    loop(5, 7, step_q)
     w.relay()
-    step_q(5)
+    step_q(7)
     w.finish()
     wide = wide_ref[...].astype(f32)
     scale = lax.rsqrt(jnp.mean(wide * wide, axis=-1, keepdims=True) + eps)
@@ -396,18 +428,14 @@
     kv_ref[y, z] = kv.astype(bf16)
     kva.own()
     kvb.own()
-    step_q(6)
     kva.spread()
 
     def step_kv(t):
         kva.step(t)
         kvb.step(t)
 
-    def step_both(t):
-        step_q(t + 6)
-        step_kv(t)
-
-    loop(1, 3, step_both)
+    step_q(8)
+    loop(1, 3, step_kv)
     qb.finish()
     queries = jnp.dot(wide_n, q_ref[...].reshape(4096, 512), preferred_element_type=f32).astype(bf16)
     stacked = jnp.concatenate([queries[:, h * HEAD : (h + 1) * HEAD] for h in range(GROUP)], 0)

time: 126 us -> 119 us (0.944); the launches traced: 124 us -> 118 us
  Pallas kernels: 122 us -> 117 us
    pallas_call x1, Pallas kernels: 122 us -> 117 us  [on_device(): pl.pallas_call(kernel, out_shape=jax.ShapeDtypeStruct((ROWS, 128), bf16),...]
where the time goes in v4:
time: 119 us; the launch traced here: 118 us
  Pallas kernels  117 us (98%)
  local copies, waits for them, and re-layouts  1.47 us (1%)
    pallas_call x1, Pallas kernels, on_device(): pl.pallas_call(kernel, out_shape=jax.ShapeDtypeStruct((ROWS, 128), bf16),...  117 us

profile of v4, /device:TPU:25, one launch (start us, length us, event | category | flops | bytes accessed | tf_op | source)
XLA Modules:
  0.0 118.4 jit_solution(9319906877256539586)
XLA Ops:
  0.0 116.9 %window.1 = bf16[256,128]{1,0:T(8,128)(2,1)} custom-call(s32[64]{0:T(128)} %counts_ref.1, s32[1,128]{1,0:T(1,128)} %marks_ref.1, f32[1024]{0:T(1024)} %gain_ref.1, f32[128]{0:T(128)} %rate_ref.1, f32[512]{0:T(512)} %bias_ref.1, f32[4096]{0:T(1024)} %igain_ref.1, bf16[256,1024]{1,0:T(8,128)(2,1)} %bytes_hbm.1, bf16[1024,128]{1,0:T(8,128)(2,1)} %win_hbm.1, ...), custom_call_target="tpu_custom_call" | custom-call | tf_op jit(solution)/shard_map/window/pallas_call | solution.py:523
  116.9 1.5 %copy.17 = bf16[256,128]{1,0:T(8,128)(2,1)} copy(bf16[256,128]{1,0:T(8,128)(2,1)} %window.1) | data formatting | bytes 131072
